TPU v7x, 256 devices: a whole 4x4x8 slice. The times are simulated.
256 devices in a mesh: row: 16 (over x, z_hi), col: 16 (over y, z_lo, core).
Axes of the slice: x: 4, y: 4, z: 8 (z_hi: 4, z_lo: 2; z = z_hi * 2 + z_lo), core: 2. Of those that a mesh axis runs over, the one named last changes fastest.
Arguments:
- tile_count: int32 [16, 16], P('row', 'col'), may hold values from 1 to 40, as said below
- tile_rows: int32 [16, 16, 40], P('row', 'col'), may hold values from 0 to 31, as said below
- tile_cols: int32 [16, 16, 40], P('row', 'col'), may hold values from 0 to 31, as said below
- tiles: float32 [16, 16, 40, 256, 256], P('row', 'col')
- block: float32 [64, 131072], P(None, ('row', 'col')), may hold values from -6 to 6
Outputs:
- image_x: float32 [64, 131072], P(None, ('row', 'col'))
- image_w: float32 [64, 131072], P(None, ('row', 'col'))
- grams: float32 [4, 64, 64], replicated
Inputs may be any that keep to these rules, and one draw needn't show every extreme that they name: `tile_count`: live slots of each grid block; the largest count over the grid is exactly 40. `tile_rows`: live slots of one grid block hold distinct positions whose global tile row is at least the global tile column; slots at or past the count hold 0. `tile_cols`: paired with tile_rows as above; slots at or past the count hold 0.
All inputs are finite; a program needn't handle non-finite values.
Results may differ from a plain program's by a relative error of at most 0.0001.
Values sent between devices are 32-bit elements; how exact they have to be, the bound alone decides.
A program may use at most 64 MiB of HBM per device.

v0:
```python
import jax
import jax.numpy as jnp
from jax import lax
from jax.sharding import PartitionSpec as P

highest = lax.Precision.HIGHEST


def passed_along(array, axis, by):
    size = lax.axis_size(axis)
    return lax.ppermute(array, axis, [(i, (i + by) % size) for i in range(size)])


def inner_prod(left, right):
    return lax.dot_general(
        left, right, (((1,), (1,)), ((), ())), precision=highest, preferred_element_type=jnp.float32
    )


def on_device(tile_count, tile_rows, tile_cols, tiles, block):
    vec_count, seg_rows = block.shape
    tile_size = tiles.shape[-1]
    seg_tiles = seg_rows // tile_size
    grid_rows = lax.axis_size("row")
    grid_cols = lax.axis_size("col")
    total_rows = seg_rows * grid_rows * grid_cols
    live_count = tile_count[0, 0]
    row_ids = tile_rows[0, 0]
    col_ids = tile_cols[0, 0]
    tile_data = tiles[0, 0]
    row_slots = grid_cols * seg_tiles
    col_slots = grid_rows * seg_tiles

    def expand(vectors):
        near_vec = lax.all_gather(vectors, "col", axis=1, tiled=True)
        far_vec = lax.all_gather(vectors, "row", axis=1, tiled=True)
        near_tiles = near_vec.reshape(vec_count, row_slots, tile_size)
        far_tiles = far_vec.reshape(vec_count, col_slots, tile_size)
        groups = (live_count + 7) // 8

        def accumulate(counter, carry):
            sums_rows, sums_cols = carry
            offset = counter * 8
            block_tiles = lax.dynamic_slice_in_dim(tile_data, offset, 8, 0)
            slot_rows = lax.dynamic_slice_in_dim(row_ids, offset, 8, 0)
            slot_cols = lax.dynamic_slice_in_dim(col_ids, offset, 8, 0)
            live_mask = (offset + jnp.arange(8, dtype=jnp.int32) < live_count).astype(jnp.float32)
            rows_in = jnp.take(near_tiles, slot_rows, axis=1)
            cols_in = jnp.take(far_tiles, slot_cols, axis=1)
            lower_part = (
                jnp.einsum("sij,ksj->ksi", block_tiles, cols_in, precision=highest)
                * live_mask[None, :, None]
            )
            upper_part = (
                jnp.einsum("sij,ksi->ksj", block_tiles, rows_in, precision=highest)
                * live_mask[None, :, None]
            )
            row_pick = (
                slot_rows[:, None] == jnp.arange(row_slots, dtype=jnp.int32)[None, :]
            ).astype(jnp.float32)
            col_pick = (
                slot_cols[:, None] == jnp.arange(col_slots, dtype=jnp.int32)[None, :]
            ).astype(jnp.float32)
            sums_rows = sums_rows + jnp.einsum(
                "ksi,sp->kpi", lower_part, row_pick, precision=highest
            )
            sums_cols = sums_cols + jnp.einsum(
                "ksi,sp->kpi", upper_part, col_pick, precision=highest
            )
            return (sums_rows, sums_cols)

        empty_rows = jnp.zeros((vec_count, row_slots, tile_size), jnp.float32)
        empty_cols = jnp.zeros((vec_count, col_slots, tile_size), jnp.float32)
        part_rows, part_cols = lax.fori_loop(0, groups, accumulate, (empty_rows, empty_cols))
        return (
            near_vec,
            far_vec,
            part_rows.reshape(vec_count, row_slots * tile_size),
            part_cols.reshape(vec_count, col_slots * tile_size),
        )

    def combine_sums(part_rows, part_cols):
        pieces_rows = part_rows.reshape(vec_count, grid_cols, seg_rows)
        pieces_cols = part_cols.reshape(vec_count, grid_rows, seg_rows)
        my_col = lax.axis_index("col")
        my_row = lax.axis_index("row")

        def select_piece(pieces, position):
            return lax.dynamic_index_in_dim(pieces, position, 1, keepdims=False)

        def pass_along_rows(counter, running):
            moved = passed_along(running, "col", 1)
            return moved + select_piece(
                pieces_rows, (my_col + 2 * grid_cols - 1 - counter) % grid_cols
            )

        def pass_along_cols(counter, running):
            moved = passed_along(running, "row", 1)
            return moved + select_piece(
                pieces_cols, (my_row + 2 * grid_rows - 1 - counter) % grid_rows
            )

        first_rows = select_piece(pieces_rows, (my_col + grid_cols - 1) % grid_cols)
        first_cols = select_piece(pieces_cols, (my_row + grid_rows - 1) % grid_rows)
        own_rows = lax.fori_loop(1, grid_cols, pass_along_rows, first_rows)
        own_cols = lax.fori_loop(1, grid_rows, pass_along_cols, first_cols)
        return own_rows + own_cols

    near_x, far_x, rows_x, cols_x = expand(block)
    image_x = combine_sums(rows_x, cols_x)
    first_term = inner_prod(block, image_x)
    rayleigh = lax.psum(first_term, ("row", "col")) / total_rows
    resid = image_x - jnp.dot(
        rayleigh, block, precision=highest, preferred_element_type=jnp.float32
    )
    near_w, far_w, rows_w, cols_w = expand(resid)
    image_w = combine_sums(rows_w, cols_w)
    cross_term = inner_prod(block, image_w)
    resid_term = inner_prod(resid, image_w)
    square_term = inner_prod(resid, resid)
    others = lax.psum(jnp.stack([cross_term, resid_term, square_term]), ("row", "col")) / total_rows
    grams = jnp.concatenate([rayleigh[None], others], axis=0)
    return (image_x, image_w, grams)


def solution(mesh):
    return jax.shard_map(
        on_device,
        mesh=mesh,
        in_specs=(
            P("row", "col"),
            P("row", "col", None),
            P("row", "col", None),
            P("row", "col", None, None, None),
            P(None, ("row", "col")),
        ),
        out_specs=(P(None, ("row", "col")), P(None, ("row", "col")), P()),
        check_vma=False,
    )
```

profile of v0, /device:TPU:1, one launch (start us, length us, event | category | flops | bytes accessed | tf_op | source)
XLA Modules:
  0.0 1077.0 jit_solution(5392531176664811493)
XLA Ops:
  9.4 40.8 %all-gather.7.cloned.1.call-done = f32[64,8192]{1,0:T(8,128)} async-done(((f32[64,512]{1,0:T(8,128)}), f32[64,8192]{1,0:T(8,128)}) %all-gather.7.cloned.1.call-update) | async-done | bytes 2097168 | tf_op jit(solution)/shard_map/all_gather | solution.py:35
  53.4 56.9 %all-gather.5.cloned.1.call-done = f32[64,8192]{1,0:T(8,128)} async-done(((f32[64,512]{1,0:T(8,128)}), f32[64,8192]{1,0:T(8,128)}) %all-gather.5.cloned.1.call-update) | async-done | bytes 2097168 | tf_op jit(solution)/shard_map/all_gather | solution.py:36
  115.4 17.8 %while.84 = (s32[]{:T(128)}, f32[64,32,256]{2,1,0:T(8,128)S(1)}, f32[64,32,256]{2,1,0:T(8,128)}, s32[]{:T(128)}, s32[40]{0:T(128)S(1)}, /*index=5*/s32[40]{0:T(1...) while((s32[]{:T(128)}, f32[64,32,256]{2,1,0:T(8,128)S(1)}, ...), condition=%wide.region_1.3_spmd, body=%wide.region_0.2_spmd.sunk | while | flops 907545280 | bytes 17834760 | solution.py:74
  140.4 217.7 %while.86 = (s32[]{:T(128)}, f32[64,512]{1,0:T(8,128)S(1)}, s32[]{:T(128)}, f32[64,16,512]{2,1,0:T(8,128)}, s32[]{:T(128)}, /*index=5*/s32[]{:T(128)}, s32[]{:T(128)}, s32[]{:T(128)}) while((s32[]{:T(128)}, f32[64,512]{1,0:T(8,128)S(1)}, s32[]{:T(128)}, f32[64,16,512]{2,1,0:T(8,128)}, s32[]{:T(128)}, /*index=5*/s32[]{:T(128)}, s32[]{:T(128)}, ...), condition=%wide.region_5.7_spmd, body=%wide.region_4.6_spmd.sunk | while | flops 32785 | bytes 1179932 | solution.py:106
  143.3 75.8 %collective-permute-done.1 = f32[64,512]{1,0:T(8,128)S(1)} collective-permute-done((f32[64,512]{1,0:T(8,128)S(1)}, f32[64,512]{1,0:T(8,128)S(1)}, u32[]{:S(2)}, u32[]{:S(2)}) %collective-permute-start.1) | collective-permute-done | bytes 131104 | tf_op jit(solution)/shard_map/while/body/eval_jaxpr/ppermute | solution.py:11
  220.6 6.7 collective-permute-done.1
  228.7 6.7 collective-permute-done.1
  236.9 7.4 collective-permute-done.1
  245.8 9.6 collective-permute-done.1
  256.9 7.4 collective-permute-done.1
  265.8 9.0 collective-permute-done.1
  276.3 9.1 collective-permute-done.1
  286.9 10.8 %collective-permute-done.1 = f32[64,512]{1,0:T(8,128)S(1)} collective-permute-done((f32[64,512]{1,0:T(8,128)S(1)}, f32[64,512]{1,0:T(8,128)S(1)}, u32[]{:S(2)}, u32[]{:S(2)}) %collective-permute-start.1) | collective-permute-done | bytes 131104 | tf_op jit(solution)/shard_map/while/body/eval_jaxpr/ppermute | solution.py:11
  299.2 9.9 collective-permute-done.1
  310.6 8.7 collective-permute-done.1
  320.8 10.4 collective-permute-done.1
  332.7 8.9 collective-permute-done.1
  343.1 6.8 collective-permute-done.1
  351.4 6.7 collective-permute-done.1
  358.1 108.0 %while.85 = (s32[]{:T(128)}, f32[64,512]{1,0:T(8,128)S(1)}, s32[]{:T(128)}, f32[64,16,512]{2,1,0:T(8,128)}, s32[]{:T(128)}, /*index=5*/s32[]{:T(128)}, s32[]{:T(128)}, s32[]{:T(128)}) while((s32[]{:T(128)}, f32[64,512]{1,0:T(8,128)S(1)}, s32[]{:T(128)}, f32[64,16,512]{2,1,0:T(8,128)}, s32[]{:T(128)}, /*index=5*/s32[]{:T(128)}, s32[]{:T(128)}, ...), condition=%wide.region_3.5_spmd, body=%wide.region_2.4_spmd.sunk | while | flops 32785 | bytes 1179932 | solution.py:105
  358.1 9.1 collective-permute-start
  374.9 5.1 collective-permute-done
  381.6 5.1 collective-permute-done
  388.2 5.1 collective-permute-done
  394.8 5.1 collective-permute-done
  466.4 76.2 %psum.14 = f32[64,64]{0,1:T(8,128)S(1)} all-reduce(f32[64,64]{0,1:T(8,128)S(1)} %convolution_bitcast_fusion.3), channel_id=1, replica_groups=mesh['row'=16,'col'=16] {'row','col'}, use_global_device_ids=true, to_apply=%region_6.8 | all-reduce | flops 4096 | bytes 32768 | tf_op jit(solution)/shard_map/psum | solution.py:112
  545.5 30.2 %all-gather.11.cloned.1.call-done = f32[64,8192]{1,0:T(8,128)} async-done(((f32[64,512]{1,0:T(8,128)}), f32[64,8192]{1,0:T(8,128)}) %all-gather.11.cloned.1.call-update) | async-done | bytes 2097168 | tf_op jit(solution)/shard_map/all_gather | solution.py:35
  578.9 57.3 %all-gather.9.cloned.1.call-done = f32[64,8192]{1,0:T(8,128)} async-done(((f32[64,512]{1,0:T(8,128)}), f32[64,8192]{1,0:T(8,128)}) %all-gather.9.cloned.1.call-update) | async-done | bytes 2097168 | tf_op jit(solution)/shard_map/all_gather | solution.py:36
  641.3 17.8 %while.87 = (s32[]{:T(128)}, f32[64,32,256]{2,1,0:T(8,128)S(1)}, f32[64,32,256]{2,1,0:T(8,128)}, s32[]{:T(128)}, s32[40]{0:T(128)S(1)}, /*index=5*/s32[40]{0:T(1...) while((s32[]{:T(128)}, f32[64,32,256]{2,1,0:T(8,128)S(1)}, ...), condition=%wide.region_8.10_spmd, body=%wide.region_7.9_spmd.sunk | while | flops 907545280 | bytes 17834760 | solution.py:74
  666.3 222.1 %while.89 = (s32[]{:T(128)}, f32[64,512]{1,0:T(8,128)S(1)}, s32[]{:T(128)}, f32[64,16,512]{2,1,0:T(8,128)}, s32[]{:T(128)}, /*index=5*/s32[]{:T(128)}, s32[]{:T(128)}, s32[]{:T(128)}) while((s32[]{:T(128)}, f32[64,512]{1,0:T(8,128)S(1)}, s32[]{:T(128)}, f32[64,16,512]{2,1,0:T(8,128)}, s32[]{:T(128)}, /*index=5*/s32[]{:T(128)}, s32[]{:T(128)}, ...), condition=%wide.region_12.14_spmd, body=%wide.region_11.13_spmd.sunk | while | flops 32785 | bytes 1179932 | solution.py:106
  669.2 75.8 %collective-permute-done.3 = f32[64,512]{1,0:T(8,128)S(1)} collective-permute-done((f32[64,512]{1,0:T(8,128)S(1)}, f32[64,512]{1,0:T(8,128)S(1)}, u32[]{:S(2)}, u32[]{:S(2)}) %collective-permute-start.3) | collective-permute-done | bytes 131104 | tf_op jit(solution)/shard_map/while/body/eval_jaxpr/ppermute | solution.py:11
  746.5 6.7 collective-permute-done.3
  754.6 6.7 collective-permute-done.3
  762.8 7.5 collective-permute-done.3
  771.8 9.6 collective-permute-done.3
  782.9 7.4 collective-permute-done.3
  791.8 9.2 collective-permute-done.3
  802.5 8.7 collective-permute-done.3
  812.7 10.7 collective-permute-done.3
  824.8 10.1 collective-permute-done.3
  836.4 8.7 collective-permute-done.3
  846.6 10.4 collective-permute-done.3
  858.6 8.6 collective-permute-done.3
  868.7 9.3 collective-permute-done.3
  879.4 8.9 collective-permute-done.3
  888.4 104.1 %while.88 = (s32[]{:T(128)}, f32[64,512]{1,0:T(8,128)S(1)}, s32[]{:T(128)}, f32[64,16,512]{2,1,0:T(8,128)}, s32[]{:T(128)}, /*index=5*/s32[]{:T(128)}, s32[]{:T(128)}, s32[]{:T(128)}) while((s32[]{:T(128)}, f32[64,512]{1,0:T(8,128)S(1)}, s32[]{:T(128)}, f32[64,16,512]{2,1,0:T(8,128)}, s32[]{:T(128)}, /*index=5*/s32[]{:T(128)}, s32[]{:T(128)}, ...), condition=%wide.region_10.12_spmd, body=%wide.region_9.11_spmd.sunk | while | flops 32785 | bytes 1179932 | solution.py:105
  894.4 5.5 collective-permute-done.2
  993.1 76.6 %psum.15 = f32[3,64,64]{1,2,0:T(8,128)S(1)} all-reduce(f32[3,64,64]{1,2,0:T(8,128)S(1)} %pad_maximum_fusion.1), channel_id=1, replica_groups=mesh['row'=16,'col'=16] {'row','col'}, use_global_device_ids=true, to_apply=%region_13.15 | all-reduce | flops 12288 | bytes 98304 | tf_op jit(solution)/shard_map/psum | solution.py:121
  (280 shorter events, 294.1 us)
Async XLA Ops:
  7.2 43.1 %all-gather.7.cloned.1.call-start = ((), (), s32[]{:S(2)}) async-start(), calls=%async_computation.1 | async-start | bytes 2228224 | tf_op jit(solution)/shard_map/all_gather | solution.py:35
  7.9 102.4 %all-gather.5.cloned.1.call-start = ((), (), s32[]{:S(2)}) async-start(), calls=%async_computation | async-start | bytes 2228224 | tf_op jit(solution)/shard_map/all_gather | solution.py:36
  8.6 567.1 %all-gather.11.cloned.1.call-start = ((), (), s32[]{:S(2)}) async-start(), calls=%async_computation.3 | async-start | bytes 2228224 | tf_op jit(solution)/shard_map/all_gather | solution.py:35
  140.4 78.7 %collective-permute-start.1 = (f32[64,512]{1,0:T(8,128)S(1)}, f32[64,512]{1,0:T(8,128)S(1)}, u32[]{:S(2)}, u32[]{:S(2)}) collective-permute-start(f32[64,512]{1,0:T(8,128)S(1)} %get-tuple-element.1050), channel_id=1, source_target_pairs={{0,16},{16,32},{32,48},{48,64},{64,80},{80,96},{96,112},{112,128},... | collective-permute-start | bytes 393224 | tf_op jit(solution)/shard_map/while/body/eval_jaxpr/ppermute | solution.py:11
  219.1 8.1 collective-permute-start.1
  227.3 8.1 collective-permute-start.1
  235.4 8.9 collective-permute-start.1
  244.4 11.1 %collective-permute-start.1 = (f32[64,512]{1,0:T(8,128)S(1)}, f32[64,512]{1,0:T(8,128)S(1)}, u32[]{:S(2)}, u32[]{:S(2)}) collective-permute-start(f32[64,512]{1,0:T(8,128)S(1)} %get-tuple-element.1050), channel_id=1, source_target_pairs={{0,16},{16,32},{32,48},{48,64},{64,80},{80,96},{96,112},{112,128},... | collective-permute-start | bytes 393224 | tf_op jit(solution)/shard_map/while/body/eval_jaxpr/ppermute | solution.py:11
  255.5 8.9 collective-permute-start.1
  264.4 10.5 collective-permute-start.1
  274.9 10.5 collective-permute-start.1
  285.4 12.3 %collective-permute-start.1 = (f32[64,512]{1,0:T(8,128)S(1)}, f32[64,512]{1,0:T(8,128)S(1)}, u32[]{:S(2)}, u32[]{:S(2)}) collective-permute-start(f32[64,512]{1,0:T(8,128)S(1)} %get-tuple-element.1050), channel_id=1, source_target_pairs={{0,16},{16,32},{32,48},{48,64},{64,80},{80,96},{96,112},{112,128},... | collective-permute-start | bytes 393224 | tf_op jit(solution)/shard_map/while/body/eval_jaxpr/ppermute | solution.py:11
  297.7 11.4 %collective-permute-start.1 = (f32[64,512]{1,0:T(8,128)S(1)}, f32[64,512]{1,0:T(8,128)S(1)}, u32[]{:S(2)}, u32[]{:S(2)}) collective-permute-start(f32[64,512]{1,0:T(8,128)S(1)} %get-tuple-element.1050), channel_id=1, source_target_pairs={{0,16},{16,32},{32,48},{48,64},{64,80},{80,96},{96,112},{112,128},... | collective-permute-start | bytes 393224 | tf_op jit(solution)/shard_map/while/body/eval_jaxpr/ppermute | solution.py:11
  309.2 10.1 collective-permute-start.1
  319.3 11.9 %collective-permute-start.1 = (f32[64,512]{1,0:T(8,128)S(1)}, f32[64,512]{1,0:T(8,128)S(1)}, u32[]{:S(2)}, u32[]{:S(2)}) collective-permute-start(f32[64,512]{1,0:T(8,128)S(1)} %get-tuple-element.1050), channel_id=1, source_target_pairs={{0,16},{16,32},{32,48},{48,64},{64,80},{80,96},{96,112},{112,128},... | collective-permute-start | bytes 393224 | tf_op jit(solution)/shard_map/while/body/eval_jaxpr/ppermute | solution.py:11
  331.3 10.3 collective-permute-start.1
  341.6 8.2 collective-permute-start.1
  349.9 8.1 collective-permute-start.1
  358.1 15.4 %collective-permute-start = (f32[64,512]{1,0:T(8,128)S(1)}, f32[64,512]{1,0:T(8,128)S(1)}, u32[]{:S(2)}, u32[]{:S(2)}) collective-permute-start(f32[64,512]{1,0:T(8,128)S(1)} %get-tuple-element.1026), channel_id=1, source_target_pairs={{0,1},{1,2},{2,3},{3,4},{4,5},{5,6},{6,7},{7,8},{8,9},{9,10},{10,1... | collective-permute-start | bytes 393224 | tf_op jit(solution)/shard_map/while/body/eval_jaxpr/ppermute | solution.py:11
  373.5 6.6 collective-permute-start
  380.1 6.6 collective-permute-start
  386.7 6.6 collective-permute-start
  393.3 6.6 collective-permute-start
  399.9 6.6 collective-permute-start
  406.6 6.6 collective-permute-start
  413.2 6.6 collective-permute-start
  419.8 6.6 collective-permute-start
  426.4 6.6 collective-permute-start
  433.0 6.6 collective-permute-start
  439.6 6.6 collective-permute-start
  446.2 6.6 collective-permute-start
  543.6 92.6 %all-gather.9.cloned.1.call-start = ((), (), s32[]{:S(2)}) async-start(), calls=%async_computation.2 | async-start | bytes 2228224 | tf_op jit(solution)/shard_map/all_gather | solution.py:36
  666.3 78.7 %collective-permute-start.3 = (f32[64,512]{1,0:T(8,128)S(1)}, f32[64,512]{1,0:T(8,128)S(1)}, u32[]{:S(2)}, u32[]{:S(2)}) collective-permute-start(f32[64,512]{1,0:T(8,128)S(1)} %get-tuple-element.1140), channel_id=1, source_target_pairs={{0,16},{16,32},{32,48},{48,64},{64,80},{80,96},{96,112},{112,128},... | collective-permute-start | bytes 393224 | tf_op jit(solution)/shard_map/while/body/eval_jaxpr/ppermute | solution.py:11
  745.0 8.1 collective-permute-start.3
  753.2 8.1 collective-permute-start.3
  761.3 8.9 collective-permute-start.3
  770.3 11.1 %collective-permute-start.3 = (f32[64,512]{1,0:T(8,128)S(1)}, f32[64,512]{1,0:T(8,128)S(1)}, u32[]{:S(2)}, u32[]{:S(2)}) collective-permute-start(f32[64,512]{1,0:T(8,128)S(1)} %get-tuple-element.1140), channel_id=1, source_target_pairs={{0,16},{16,32},{32,48},{48,64},{64,80},{80,96},{96,112},{112,128},... | collective-permute-start | bytes 393224 | tf_op jit(solution)/shard_map/while/body/eval_jaxpr/ppermute | solution.py:11
  781.4 8.9 collective-permute-start.3
  790.3 10.7 collective-permute-start.3
  801.0 10.1 collective-permute-start.3
  811.2 12.1 %collective-permute-start.3 = (f32[64,512]{1,0:T(8,128)S(1)}, f32[64,512]{1,0:T(8,128)S(1)}, u32[]{:S(2)}, u32[]{:S(2)}) collective-permute-start(f32[64,512]{1,0:T(8,128)S(1)} %get-tuple-element.1140), channel_id=1, source_target_pairs={{0,16},{16,32},{32,48},{48,64},{64,80},{80,96},{96,112},{112,128},... | collective-permute-start | bytes 393224 | tf_op jit(solution)/shard_map/while/body/eval_jaxpr/ppermute | solution.py:11
  823.4 11.5 %collective-permute-start.3 = (f32[64,512]{1,0:T(8,128)S(1)}, f32[64,512]{1,0:T(8,128)S(1)}, u32[]{:S(2)}, u32[]{:S(2)}) collective-permute-start(f32[64,512]{1,0:T(8,128)S(1)} %get-tuple-element.1140), channel_id=1, source_target_pairs={{0,16},{16,32},{32,48},{48,64},{64,80},{80,96},{96,112},{112,128},... | collective-permute-start | bytes 393224 | tf_op jit(solution)/shard_map/while/body/eval_jaxpr/ppermute | solution.py:11
  834.9 10.2 collective-permute-start.3
  845.2 11.9 %collective-permute-start.3 = (f32[64,512]{1,0:T(8,128)S(1)}, f32[64,512]{1,0:T(8,128)S(1)}, u32[]{:S(2)}, u32[]{:S(2)}) collective-permute-start(f32[64,512]{1,0:T(8,128)S(1)} %get-tuple-element.1140), channel_id=1, source_target_pairs={{0,16},{16,32},{32,48},{48,64},{64,80},{80,96},{96,112},{112,128},... | collective-permute-start | bytes 393224 | tf_op jit(solution)/shard_map/while/body/eval_jaxpr/ppermute | solution.py:11
  857.1 10.1 collective-permute-start.3
  867.2 10.7 collective-permute-start.3
  878.0 10.4 collective-permute-start.3
  888.4 11.5 %collective-permute-start.2 = (f32[64,512]{1,0:T(8,128)S(1)}, f32[64,512]{1,0:T(8,128)S(1)}, u32[]{:S(2)}, u32[]{:S(2)}) collective-permute-start(f32[64,512]{1,0:T(8,128)S(1)} %get-tuple-element.1116), channel_id=1, source_target_pairs={{0,1},{1,2},{2,3},{3,4},{4,5},{5,6},{6,7},{7,8},{8,9},{9,10},{10,1... | collective-permute-start | bytes 393224 | tf_op jit(solution)/shard_map/while/body/eval_jaxpr/ppermute | solution.py:11
  (22 other events, 511.9 us)
Sparse Core Ops, SparseCore 0:
  9.8 40.3 all-gather.6
  52.7 57.5 all-gather.4
  543.8 31.9 all-gather.10
  578.6 57.5 all-gather.8
where the time goes:
time: 1080 us
  waiting for transfers between devices  733 us (68%)
  blocking collectives  153 us (14%)
  local copies, waits for them, and re-layouts  121 us (11%)
  matrix products  28.2 us (3%)
  starting transfers between devices  21.7 us (2%)
  between operations  14.7 us (1%)
    ppermute x60, waiting for transfers between devices, passed_along(): lax.ppermute(array, axis, [(i, (i + by) % size) for i in range(size)])  546 us
    all_gather x2, waiting for transfers between devices, expand(): far_vec = lax.all_gather(vectors, 'row', axis=1, tiled=True)  114 us
    dynamic_slice x64, local copies, waits for them, and re-layouts, select_piece(): return lax.dynamic_index_in_dim(pieces, position, 1, keepdims=False)  85.8 us
    psum x1, blocking collectives, on_device(): lax.psum(jnp.stack([cross_term, resid_term, square_term]), ('row', 'col'))  76.6 us
    psum x1, blocking collectives, on_device(): rayleigh = lax.psum(first_term, ('row', 'col')) / total_rows  76.2 us
    all_gather x2, waiting for transfers between devices, expand(): near_vec = lax.all_gather(vectors, 'col', axis=1, tiled=True)  71.1 us
  transfers between devices with their start and end apart: 64, of which 64 were waited for; matrix products, arithmetic and copies ran while one was open for 8% of the time, Pallas kernels for 0%

commit v1 on v0

--- a/solution.py
+++ b/solution.py
@@ -33,7 +33,9 @@
 
     def expand(vectors):
         near_vec = lax.all_gather(vectors, "col", axis=1, tiled=True)
-        far_vec = lax.all_gather(vectors, "row", axis=1, tiled=True)
+        far_vec = jnp.concatenate(
+            lax.all_to_all(jnp.stack([vectors] * lax.axis_size("row")), "row", 0, 0), axis=1
+        )
         near_tiles = near_vec.reshape(vec_count, row_slots, tile_size)
         far_tiles = far_vec.reshape(vec_count, col_slots, tile_size)
         groups = (live_count + 7) // 8

time: 1080 us -> 1040 us (0.963)
  waiting for transfers between devices: 733 us -> 644 us
  starting transfers between devices: 21.7 us -> 62.1 us
  local copies, waits for them, and re-layouts: 121 us -> 132 us
    all_to_all x0 -> x2, waiting for transfers between devices: none -> 118 us  [expand(): lax.all_to_all(jnp.stack([vectors] * lax.axis_size('row')), 'row', 0, 0)]
    all_gather x2 -> x0, waiting for transfers between devices: 114 us -> none  [expand(): far_vec = lax.all_gather(vectors, 'row', axis=1, tiled=True)]
    all_gather x2, waiting for transfers between devices: 71.1 us -> 0.01 us  [expand(): near_vec = lax.all_gather(vectors, 'col', axis=1, tiled=True)]
    ppermute x60, starting transfers between devices: 21.6 us -> 45.8 us  [passed_along(): lax.ppermute(array, axis, [(i, (i + by) % size) for i in range(size)])]
    ppermute x60, waiting for transfers between devices: 546 us -> 525 us  [passed_along(): lax.ppermute(array, axis, [(i, (i + by) % size) for i in range(size)])]
    all_to_all x0 -> x2, starting transfers between devices: none -> 16.2 us  [expand(): lax.all_to_all(jnp.stack([vectors] * lax.axis_size('row')), 'row', 0, 0)]
  transfers between devices with their start and end apart: 64 -> 64, of which waited for: 64 -> 62; matrix products, arithmetic and copies ran while one was open for 8% -> 9% of each run, Pallas kernels for 0% -> 0%
where the time goes in v1:
time: 1040 us
  waiting for transfers between devices  644 us (62%)
  blocking collectives  153 us (15%)
  local copies, waits for them, and re-layouts  132 us (13%)
  starting transfers between devices  62.1 us (6%)
  matrix products  27.6 us (3%)
  between operations  15 us (1%)
    ppermute x60, waiting for transfers between devices, passed_along(): lax.ppermute(array, axis, [(i, (i + by) % size) for i in range(size)])  525 us
    all_to_all x2, waiting for transfers between devices, expand(): lax.all_to_all(jnp.stack([vectors] * lax.axis_size('row')), 'row', 0, 0)  118 us
    dynamic_slice x64, local copies, waits for them, and re-layouts, select_piece(): return lax.dynamic_index_in_dim(pieces, position, 1, keepdims=False)  85.8 us
    psum x1, blocking collectives, on_device(): lax.psum(jnp.stack([cross_term, resid_term, square_term]), ('row', 'col'))  76.6 us
    psum x1, blocking collectives, on_device(): rayleigh = lax.psum(first_term, ('row', 'col')) / total_rows  76.2 us
    ppermute x60, starting transfers between devices, passed_along(): lax.ppermute(array, axis, [(i, (i + by) % size) for i in range(size)])  45.8 us
  transfers between devices with their start and end apart: 64, of which 62 were waited for; matrix products, arithmetic and copies ran while one was open for 9% of the time, Pallas kernels for 0%

profile of v1, /device:TPU:1, one launch (start us, length us, event | category | flops | bytes accessed | tf_op | source)
XLA Modules:
  0.0 1039.5 jit_solution(14946685328093138639)
XLA Ops:
  9.7 11.6 %all-to-all-start = ((f32[16,64,512]{2,1,0:T(8,128)}), f32[16,64,512]{2,1,0:T(8,128)S(1)}, u32[]{:S(2)}, u32[]{:S(2)}) async-start(f32[16,64,512]{2,1,0:T(8,128)} %stack.12), calls=%async_computation | async-start | bytes 4194304 | tf_op jit(solution)/shard_map/all_to_all | solution.py:37
  22.7 58.7 %all-to-all-done = f32[16,64,512]{2,1,0:T(8,128)S(1)} async-done(((f32[16,64,512]{2,1,0:T(8,128)}), f32[16,64,512]{2,1,0:T(8,128)S(1)}, u32[]{:S(2)}, u32[]{:S(2)}) %all-to-all-start) | async-done | bytes 2097184 | tf_op jit(solution)/shard_map/all_to_all | solution.py:37
  93.3 17.9 %while.84 = (s32[]{:T(128)}, f32[64,32,256]{2,1,0:T(8,128)S(1)}, f32[64,32,256]{2,1,0:T(8,128)}, s32[]{:T(128)}, s32[40]{0:T(128)S(1)}, /*index=5*/s32[40]{0:T(1...) while((s32[]{:T(128)}, f32[64,32,256]{2,1,0:T(8,128)S(1)}, ...), condition=%wide.region_1.3_spmd, body=%wide.region_0.2_spmd.sunk | while | flops 907545280 | bytes 17834760 | solution.py:76
  118.4 221.1 %while.86 = (s32[]{:T(128)}, f32[64,512]{1,0:T(8,128)S(1)}, s32[]{:T(128)}, f32[64,16,512]{2,1,0:T(8,128)}, s32[]{:T(128)}, /*index=5*/s32[]{:T(128)}, s32[]{:T(128)}, s32[]{:T(128)}) while((s32[]{:T(128)}, f32[64,512]{1,0:T(8,128)S(1)}, s32[]{:T(128)}, f32[64,16,512]{2,1,0:T(8,128)}, s32[]{:T(128)}, /*index=5*/s32[]{:T(128)}, s32[]{:T(128)}, ...), condition=%wide.region_5.7_spmd, body=%wide.region_4.6_spmd.sunk | while | flops 32785 | bytes 1179932 | solution.py:108
  120.5 77.9 %collective-permute-done.1 = f32[64,512]{1,0:T(8,128)S(1)} collective-permute-done((f32[64,512]{1,0:T(8,128)S(1)}, f32[64,512]{1,0:T(8,128)S(1)}, u32[]{:S(2)}, u32[]{:S(2)}) %collective-permute-start.1) | collective-permute-done | bytes 131104 | tf_op jit(solution)/shard_map/while/body/eval_jaxpr/ppermute | solution.py:11
  199.9 7.2 collective-permute-done.1
  208.7 8.2 collective-permute-done.1
  218.4 7.5 collective-permute-done.1
  227.4 9.6 collective-permute-done.1
  238.4 9.5 collective-permute-done.1
  249.4 10.3 collective-permute-done.1
  261.2 6.9 collective-permute-done.1
  269.6 6.7 collective-permute-done.1
  277.7 6.8 collective-permute-done.1
  286.0 7.6 collective-permute-done.1
  295.1 9.6 collective-permute-done.1
  306.2 9.1 collective-permute-done.1
  316.8 10.4 collective-permute-done.1
  328.7 10.8 %collective-permute-done.1 = f32[64,512]{1,0:T(8,128)S(1)} collective-permute-done((f32[64,512]{1,0:T(8,128)S(1)}, f32[64,512]{1,0:T(8,128)S(1)}, u32[]{:S(2)}, u32[]{:S(2)}) %collective-permute-start.1) | collective-permute-done | bytes 131104 | tf_op jit(solution)/shard_map/while/body/eval_jaxpr/ppermute | solution.py:11
  339.6 105.6 %while.85 = (s32[]{:T(128)}, f32[64,512]{1,0:T(8,128)S(1)}, s32[]{:T(128)}, f32[64,16,512]{2,1,0:T(8,128)}, s32[]{:T(128)}, /*index=5*/s32[]{:T(128)}, s32[]{:T(128)}, s32[]{:T(128)}) while((s32[]{:T(128)}, f32[64,512]{1,0:T(8,128)S(1)}, s32[]{:T(128)}, f32[64,16,512]{2,1,0:T(8,128)}, s32[]{:T(128)}, /*index=5*/s32[]{:T(128)}, s32[]{:T(128)}, ...), condition=%wide.region_3.5_spmd, body=%wide.region_2.4_spmd.sunk | while | flops 32785 | bytes 1179932 | solution.py:107
  339.6 13.1 %collective-permute-start = (f32[64,512]{1,0:T(8,128)S(1)}, f32[64,512]{1,0:T(8,128)S(1)}, u32[]{:S(2)}, u32[]{:S(2)}) collective-permute-start(f32[64,512]{1,0:T(8,128)S(1)} %get-tuple-element.1065), channel_id=1, source_target_pairs={{0,1},{1,2},{2,3},{3,4},{4,5},{5,6},{6,7},{7,8},{8,9},{9,10},{10,1... | collective-permute-start | bytes 393224 | tf_op jit(solution)/shard_map/while/body/eval_jaxpr/ppermute | solution.py:11
  373.9 5.1 collective-permute-done
  380.5 5.1 collective-permute-done
  387.1 5.1 collective-permute-done
  393.7 5.1 collective-permute-done
  400.3 5.1 collective-permute-done
  445.5 76.2 %psum.14 = f32[64,64]{0,1:T(8,128)S(1)} all-reduce(f32[64,64]{0,1:T(8,128)S(1)} %convolution_bitcast_fusion.3), channel_id=1, replica_groups=mesh['row'=16,'col'=16] {'row','col'}, use_global_device_ids=true, to_apply=%region_6.8 | all-reduce | flops 4096 | bytes 32768 | tf_op jit(solution)/shard_map/psum | solution.py:114
  530.3 58.8 %all-to-all-done.1 = f32[16,64,512]{2,1,0:T(8,128)S(1)} async-done(((f32[16,64,512]{2,1,0:T(8,128)}), f32[16,64,512]{2,1,0:T(8,128)S(1)}, u32[]{:S(2)}, u32[]{:S(2)}) %all-to-all-start.1) | async-done | bytes 2097184 | tf_op jit(solution)/shard_map/all_to_all | solution.py:37
  600.9 17.8 %while.87 = (s32[]{:T(128)}, f32[64,32,256]{2,1,0:T(8,128)S(1)}, f32[64,32,256]{2,1,0:T(8,128)}, s32[]{:T(128)}, s32[40]{0:T(128)S(1)}, /*index=5*/s32[40]{0:T(1...) while((s32[]{:T(128)}, f32[64,32,256]{2,1,0:T(8,128)S(1)}, ...), condition=%wide.region_8.10_spmd, body=%wide.region_7.9_spmd.sunk | while | flops 907545280 | bytes 17834760 | solution.py:76
  625.9 225.1 %while.89 = (s32[]{:T(128)}, f32[64,512]{1,0:T(8,128)S(1)}, s32[]{:T(128)}, f32[64,16,512]{2,1,0:T(8,128)}, s32[]{:T(128)}, /*index=5*/s32[]{:T(128)}, s32[]{:T(128)}, s32[]{:T(128)}) while((s32[]{:T(128)}, f32[64,512]{1,0:T(8,128)S(1)}, s32[]{:T(128)}, f32[64,16,512]{2,1,0:T(8,128)}, s32[]{:T(128)}, /*index=5*/s32[]{:T(128)}, s32[]{:T(128)}, ...), condition=%wide.region_12.14_spmd, body=%wide.region_11.13_spmd.sunk | while | flops 32785 | bytes 1179932 | solution.py:108
  627.3 77.3 %collective-permute-done.3 = f32[64,512]{1,0:T(8,128)S(1)} collective-permute-done((f32[64,512]{1,0:T(8,128)S(1)}, f32[64,512]{1,0:T(8,128)S(1)}, u32[]{:S(2)}, u32[]{:S(2)}) %collective-permute-start.3) | collective-permute-done | bytes 131104 | tf_op jit(solution)/shard_map/while/body/eval_jaxpr/ppermute | solution.py:11
  706.2 10.5 %collective-permute-done.3 = f32[64,512]{1,0:T(8,128)S(1)} collective-permute-done((f32[64,512]{1,0:T(8,128)S(1)}, f32[64,512]{1,0:T(8,128)S(1)}, u32[]{:S(2)}, u32[]{:S(2)}) %collective-permute-start.3) | collective-permute-done | bytes 131104 | tf_op jit(solution)/shard_map/while/body/eval_jaxpr/ppermute | solution.py:11
  718.1 10.1 collective-permute-done.3
  729.7 10.0 collective-permute-done.3
  741.1 8.8 collective-permute-done.3
  751.4 9.7 collective-permute-done.3
  762.6 6.7 collective-permute-done.3
  770.7 6.7 collective-permute-done.3
  778.9 6.7 collective-permute-done.3
  787.0 8.5 collective-permute-done.3
  797.1 10.4 collective-permute-done.3
  809.0 6.7 collective-permute-done.3
  817.2 10.0 collective-permute-done.3
  828.6 9.8 collective-permute-done.3
  839.9 11.0 %collective-permute-done.3 = f32[64,512]{1,0:T(8,128)S(1)} collective-permute-done((f32[64,512]{1,0:T(8,128)S(1)}, f32[64,512]{1,0:T(8,128)S(1)}, u32[]{:S(2)}, u32[]{:S(2)}) %collective-permute-start.3) | collective-permute-done | bytes 131104 | tf_op jit(solution)/shard_map/while/body/eval_jaxpr/ppermute | solution.py:11
  850.9 103.7 %while.88 = (s32[]{:T(128)}, f32[64,512]{1,0:T(8,128)S(1)}, s32[]{:T(128)}, f32[64,16,512]{2,1,0:T(8,128)}, s32[]{:T(128)}, /*index=5*/s32[]{:T(128)}, s32[]{:T(128)}, s32[]{:T(128)}) while((s32[]{:T(128)}, f32[64,512]{1,0:T(8,128)S(1)}, s32[]{:T(128)}, f32[64,16,512]{2,1,0:T(8,128)}, s32[]{:T(128)}, /*index=5*/s32[]{:T(128)}, s32[]{:T(128)}, ...), condition=%wide.region_10.12_spmd, body=%wide.region_9.11_spmd.sunk | while | flops 32785 | bytes 1179932 | solution.py:107
  851.0 13.8 %collective-permute-start.2 = (f32[64,512]{1,0:T(8,128)S(1)}, f32[64,512]{1,0:T(8,128)S(1)}, u32[]{:S(2)}, u32[]{:S(2)}) collective-permute-start(f32[64,512]{1,0:T(8,128)S(1)} %get-tuple-element.1155), channel_id=1, source_target_pairs={{0,1},{1,2},{2,3},{3,4},{4,5},{5,6},{6,7},{7,8},{8,9},{9,10},{10,1... | collective-permute-start | bytes 393224 | tf_op jit(solution)/shard_map/while/body/eval_jaxpr/ppermute | solution.py:11
  955.3 76.6 %psum.15 = f32[3,64,64]{1,2,0:T(8,128)S(1)} all-reduce(f32[3,64,64]{1,2,0:T(8,128)S(1)} %pad_maximum_fusion.1), channel_id=1, replica_groups=mesh['row'=16,'col'=16] {'row','col'}, use_global_device_ids=true, to_apply=%region_13.15 | all-reduce | flops 12288 | bytes 98304 | tf_op jit(solution)/shard_map/psum | solution.py:123
  (286 shorter events, 286.3 us)
Async XLA Ops:
  9.7 71.7 %all-to-all-start = ((f32[16,64,512]{2,1,0:T(8,128)}), f32[16,64,512]{2,1,0:T(8,128)S(1)}, u32[]{:S(2)}, u32[]{:S(2)}) async-start(f32[16,64,512]{2,1,0:T(8,128)} %stack.12), calls=%async_computation | async-start | bytes 4194304 | tf_op jit(solution)/shard_map/all_to_all | solution.py:37
  21.2 67.0 %all-gather.3.cloned.1.call-start = ((), (), s32[]{:S(2)}) async-start(), calls=%async_computation.2 | async-start | bytes 2228224 | tf_op jit(solution)/shard_map/all_gather | solution.py:35
  118.4 80.0 %collective-permute-start.1 = (f32[64,512]{1,0:T(8,128)S(1)}, f32[64,512]{1,0:T(8,128)S(1)}, u32[]{:S(2)}, u32[]{:S(2)}) collective-permute-start(f32[64,512]{1,0:T(8,128)S(1)} %get-tuple-element.1089), channel_id=1, source_target_pairs={{0,16},{16,32},{32,48},{48,64},{64,80},{80,96},{96,112},{112,128},... | collective-permute-start | bytes 393224 | tf_op jit(solution)/shard_map/while/body/eval_jaxpr/ppermute | solution.py:11
  198.5 8.7 collective-permute-start.1
  207.2 9.7 collective-permute-start.1
  216.9 9.0 collective-permute-start.1
  225.9 11.0 %collective-permute-start.1 = (f32[64,512]{1,0:T(8,128)S(1)}, f32[64,512]{1,0:T(8,128)S(1)}, u32[]{:S(2)}, u32[]{:S(2)}) collective-permute-start(f32[64,512]{1,0:T(8,128)S(1)} %get-tuple-element.1089), channel_id=1, source_target_pairs={{0,16},{16,32},{32,48},{48,64},{64,80},{80,96},{96,112},{112,128},... | collective-permute-start | bytes 393224 | tf_op jit(solution)/shard_map/while/body/eval_jaxpr/ppermute | solution.py:11
  237.0 10.9 %collective-permute-start.1 = (f32[64,512]{1,0:T(8,128)S(1)}, f32[64,512]{1,0:T(8,128)S(1)}, u32[]{:S(2)}, u32[]{:S(2)}) collective-permute-start(f32[64,512]{1,0:T(8,128)S(1)} %get-tuple-element.1089), channel_id=1, source_target_pairs={{0,16},{16,32},{32,48},{48,64},{64,80},{80,96},{96,112},{112,128},... | collective-permute-start | bytes 393224 | tf_op jit(solution)/shard_map/while/body/eval_jaxpr/ppermute | solution.py:11
  247.9 11.8 %collective-permute-start.1 = (f32[64,512]{1,0:T(8,128)S(1)}, f32[64,512]{1,0:T(8,128)S(1)}, u32[]{:S(2)}, u32[]{:S(2)}) collective-permute-start(f32[64,512]{1,0:T(8,128)S(1)} %get-tuple-element.1089), channel_id=1, source_target_pairs={{0,16},{16,32},{32,48},{48,64},{64,80},{80,96},{96,112},{112,128},... | collective-permute-start | bytes 393224 | tf_op jit(solution)/shard_map/while/body/eval_jaxpr/ppermute | solution.py:11
  259.8 8.3 collective-permute-start.1
  268.1 8.1 collective-permute-start.1
  276.3 8.2 collective-permute-start.1
  284.5 9.1 collective-permute-start.1
  293.6 11.1 %collective-permute-start.1 = (f32[64,512]{1,0:T(8,128)S(1)}, f32[64,512]{1,0:T(8,128)S(1)}, u32[]{:S(2)}, u32[]{:S(2)}) collective-permute-start(f32[64,512]{1,0:T(8,128)S(1)} %get-tuple-element.1089), channel_id=1, source_target_pairs={{0,16},{16,32},{32,48},{48,64},{64,80},{80,96},{96,112},{112,128},... | collective-permute-start | bytes 393224 | tf_op jit(solution)/shard_map/while/body/eval_jaxpr/ppermute | solution.py:11
  304.7 10.6 %collective-permute-start.1 = (f32[64,512]{1,0:T(8,128)S(1)}, f32[64,512]{1,0:T(8,128)S(1)}, u32[]{:S(2)}, u32[]{:S(2)}) collective-permute-start(f32[64,512]{1,0:T(8,128)S(1)} %get-tuple-element.1089), channel_id=1, source_target_pairs={{0,16},{16,32},{32,48},{48,64},{64,80},{80,96},{96,112},{112,128},... | collective-permute-start | bytes 393224 | tf_op jit(solution)/shard_map/while/body/eval_jaxpr/ppermute | solution.py:11
  315.4 11.8 %collective-permute-start.1 = (f32[64,512]{1,0:T(8,128)S(1)}, f32[64,512]{1,0:T(8,128)S(1)}, u32[]{:S(2)}, u32[]{:S(2)}) collective-permute-start(f32[64,512]{1,0:T(8,128)S(1)} %get-tuple-element.1089), channel_id=1, source_target_pairs={{0,16},{16,32},{32,48},{48,64},{64,80},{80,96},{96,112},{112,128},... | collective-permute-start | bytes 393224 | tf_op jit(solution)/shard_map/while/body/eval_jaxpr/ppermute | solution.py:11
  327.2 12.3 %collective-permute-start.1 = (f32[64,512]{1,0:T(8,128)S(1)}, f32[64,512]{1,0:T(8,128)S(1)}, u32[]{:S(2)}, u32[]{:S(2)}) collective-permute-start(f32[64,512]{1,0:T(8,128)S(1)} %get-tuple-element.1089), channel_id=1, source_target_pairs={{0,16},{16,32},{32,48},{48,64},{64,80},{80,96},{96,112},{112,128},... | collective-permute-start | bytes 393224 | tf_op jit(solution)/shard_map/while/body/eval_jaxpr/ppermute | solution.py:11
  339.6 15.1 %collective-permute-start = (f32[64,512]{1,0:T(8,128)S(1)}, f32[64,512]{1,0:T(8,128)S(1)}, u32[]{:S(2)}, u32[]{:S(2)}) collective-permute-start(f32[64,512]{1,0:T(8,128)S(1)} %get-tuple-element.1065), channel_id=1, source_target_pairs={{0,1},{1,2},{2,3},{3,4},{4,5},{5,6},{6,7},{7,8},{8,9},{9,10},{10,1... | collective-permute-start | bytes 393224 | tf_op jit(solution)/shard_map/while/body/eval_jaxpr/ppermute | solution.py:11
  365.8 6.6 collective-permute-start
  372.4 6.6 collective-permute-start
  379.0 6.6 collective-permute-start
  385.6 6.6 collective-permute-start
  392.2 6.6 collective-permute-start
  398.9 6.6 collective-permute-start
  405.5 6.6 collective-permute-start
  412.1 6.6 collective-permute-start
  418.7 6.6 collective-permute-start
  425.3 6.6 collective-permute-start
  431.9 6.6 collective-permute-start
  438.5 6.6 collective-permute-start
  523.6 65.4 %all-to-all-start.1 = ((f32[16,64,512]{2,1,0:T(8,128)}), f32[16,64,512]{2,1,0:T(8,128)S(1)}, u32[]{:S(2)}, u32[]{:S(2)}) async-start(f32[16,64,512]{2,1,0:T(8,128)} %stack.13), calls=%async_computation.1 | async-start | bytes 4194304 | tf_op jit(solution)/shard_map/all_to_all | solution.py:37
  528.2 67.6 %all-gather.5.cloned.1.call-start = ((), (), s32[]{:S(2)}) async-start(), calls=%async_computation.3 | async-start | bytes 2228224 | tf_op jit(solution)/shard_map/all_gather | solution.py:35
  625.9 78.8 %collective-permute-start.3 = (f32[64,512]{1,0:T(8,128)S(1)}, f32[64,512]{1,0:T(8,128)S(1)}, u32[]{:S(2)}, u32[]{:S(2)}) collective-permute-start(f32[64,512]{1,0:T(8,128)S(1)} %get-tuple-element.1179), channel_id=1, source_target_pairs={{0,16},{16,32},{32,48},{48,64},{64,80},{80,96},{96,112},{112,128},... | collective-permute-start | bytes 393224 | tf_op jit(solution)/shard_map/while/body/eval_jaxpr/ppermute | solution.py:11
  704.7 11.9 %collective-permute-start.3 = (f32[64,512]{1,0:T(8,128)S(1)}, f32[64,512]{1,0:T(8,128)S(1)}, u32[]{:S(2)}, u32[]{:S(2)}) collective-permute-start(f32[64,512]{1,0:T(8,128)S(1)} %get-tuple-element.1179), channel_id=1, source_target_pairs={{0,16},{16,32},{32,48},{48,64},{64,80},{80,96},{96,112},{112,128},... | collective-permute-start | bytes 393224 | tf_op jit(solution)/shard_map/while/body/eval_jaxpr/ppermute | solution.py:11
  716.7 11.5 %collective-permute-start.3 = (f32[64,512]{1,0:T(8,128)S(1)}, f32[64,512]{1,0:T(8,128)S(1)}, u32[]{:S(2)}, u32[]{:S(2)}) collective-permute-start(f32[64,512]{1,0:T(8,128)S(1)} %get-tuple-element.1179), channel_id=1, source_target_pairs={{0,16},{16,32},{32,48},{48,64},{64,80},{80,96},{96,112},{112,128},... | collective-permute-start | bytes 393224 | tf_op jit(solution)/shard_map/while/body/eval_jaxpr/ppermute | solution.py:11
  728.2 11.4 %collective-permute-start.3 = (f32[64,512]{1,0:T(8,128)S(1)}, f32[64,512]{1,0:T(8,128)S(1)}, u32[]{:S(2)}, u32[]{:S(2)}) collective-permute-start(f32[64,512]{1,0:T(8,128)S(1)} %get-tuple-element.1179), channel_id=1, source_target_pairs={{0,16},{16,32},{32,48},{48,64},{64,80},{80,96},{96,112},{112,128},... | collective-permute-start | bytes 393224 | tf_op jit(solution)/shard_map/while/body/eval_jaxpr/ppermute | solution.py:11
  739.7 10.2 collective-permute-start.3
  749.9 11.1 %collective-permute-start.3 = (f32[64,512]{1,0:T(8,128)S(1)}, f32[64,512]{1,0:T(8,128)S(1)}, u32[]{:S(2)}, u32[]{:S(2)}) collective-permute-start(f32[64,512]{1,0:T(8,128)S(1)} %get-tuple-element.1179), channel_id=1, source_target_pairs={{0,16},{16,32},{32,48},{48,64},{64,80},{80,96},{96,112},{112,128},... | collective-permute-start | bytes 393224 | tf_op jit(solution)/shard_map/while/body/eval_jaxpr/ppermute | solution.py:11
  761.1 8.2 collective-permute-start.3
  769.3 8.1 collective-permute-start.3
  777.4 8.1 collective-permute-start.3
  785.6 10.0 collective-permute-start.3
  795.6 11.9 %collective-permute-start.3 = (f32[64,512]{1,0:T(8,128)S(1)}, f32[64,512]{1,0:T(8,128)S(1)}, u32[]{:S(2)}, u32[]{:S(2)}) collective-permute-start(f32[64,512]{1,0:T(8,128)S(1)} %get-tuple-element.1179), channel_id=1, source_target_pairs={{0,16},{16,32},{32,48},{48,64},{64,80},{80,96},{96,112},{112,128},... | collective-permute-start | bytes 393224 | tf_op jit(solution)/shard_map/while/body/eval_jaxpr/ppermute | solution.py:11
  807.5 8.2 collective-permute-start.3
  815.7 11.4 %collective-permute-start.3 = (f32[64,512]{1,0:T(8,128)S(1)}, f32[64,512]{1,0:T(8,128)S(1)}, u32[]{:S(2)}, u32[]{:S(2)}) collective-permute-start(f32[64,512]{1,0:T(8,128)S(1)} %get-tuple-element.1179), channel_id=1, source_target_pairs={{0,16},{16,32},{32,48},{48,64},{64,80},{80,96},{96,112},{112,128},... | collective-permute-start | bytes 393224 | tf_op jit(solution)/shard_map/while/body/eval_jaxpr/ppermute | solution.py:11
  827.2 11.2 %collective-permute-start.3 = (f32[64,512]{1,0:T(8,128)S(1)}, f32[64,512]{1,0:T(8,128)S(1)}, u32[]{:S(2)}, u32[]{:S(2)}) collective-permute-start(f32[64,512]{1,0:T(8,128)S(1)} %get-tuple-element.1179), channel_id=1, source_target_pairs={{0,16},{16,32},{32,48},{48,64},{64,80},{80,96},{96,112},{112,128},... | collective-permute-start | bytes 393224 | tf_op jit(solution)/shard_map/while/body/eval_jaxpr/ppermute | solution.py:11
  838.4 12.5 %collective-permute-start.3 = (f32[64,512]{1,0:T(8,128)S(1)}, f32[64,512]{1,0:T(8,128)S(1)}, u32[]{:S(2)}, u32[]{:S(2)}) collective-permute-start(f32[64,512]{1,0:T(8,128)S(1)} %get-tuple-element.1179), channel_id=1, source_target_pairs={{0,16},{16,32},{32,48},{48,64},{64,80},{80,96},{96,112},{112,128},... | collective-permute-start | bytes 393224 | tf_op jit(solution)/shard_map/while/body/eval_jaxpr/ppermute | solution.py:11
  851.0 15.8 %collective-permute-start.2 = (f32[64,512]{1,0:T(8,128)S(1)}, f32[64,512]{1,0:T(8,128)S(1)}, u32[]{:S(2)}, u32[]{:S(2)}) collective-permute-start(f32[64,512]{1,0:T(8,128)S(1)} %get-tuple-element.1155), channel_id=1, source_target_pairs={{0,1},{1,2},{2,3},{3,4},{4,5},{5,6},{6,7},{7,8},{8,9},{9,10},{10,1... | collective-permute-start | bytes 393224 | tf_op jit(solution)/shard_map/while/body/eval_jaxpr/ppermute | solution.py:11
  (23 other events, 469.6 us)
Sparse Core Ops, SparseCore 0:
  23.8 52.5 all-gather.2
  531.4 51.1 all-gather.4
